TPU v7x, 32 devices: a whole 2x2x4 slice. The times are simulated.
32 devices in a mesh: groups: 2 (over y), row: 4 (over x, core), col: 4 (over z).
Axes of the slice: x: 2, y: 2, z: 4, core: 2. Of those that a mesh axis runs over, the one named last changes fastest.
Arguments:
- right_sides: float32 [32, 16384], P(None, ('groups', 'row')), parts along dimension 1
- nugget: float32 [16384], P(('groups', 'row')), parts along dimension 0, may hold values from 1 to 4
- cov_blocks: bfloat16 [8, 4, 32, 256, 256], P(('groups', 'row'), 'col'), parts along dimension 0
- block_rows: int32 [8, 4, 32], P(('groups', 'row'), 'col'), parts along dimension 0, may hold values from 0 to 7, as said below
- block_cols: int32 [8, 4, 32], P(('groups', 'row'), 'col'), parts along dimension 0, may hold values from 0 to 7, as said below
- block_count: int32 [8, 4], P(('groups', 'row'), 'col'), parts along dimension 0, may hold values from 4 to 32, as said below
Outputs:
- solution: float32 [32, 16384], P(None, ('groups', 'row')), parts along dimension 1
- residual: float32 [32, 16384], P(None, ('groups', 'row')), parts along dimension 1
There are 2 independent parts, one for each index of `groups`. A program takes and returns all parts, laid end to end along the dimension named above; each array names one. Nothing has to cross between parts.
Inputs may be any that keep to these rules, and one draw needn't show every extreme that they name: On each device the pairs (block_rows, block_cols) of all 32 slots are distinct; no stored block position of a problem is the mirror image of another (no pair is stored both as (g, h) and as (h, g)); on devices whose row and col index are equal, block_rows <= block_cols. `block_cols`: see block_rows. `block_count`: slots at or beyond the count are empty; some device of every problem has exactly 32 live slots.
All inputs are finite; a program needn't handle non-finite values.
Results may differ from a plain program's by a relative error of at most 0.0003.
Values sent between devices are 32-bit elements; how exact they have to be, the bound alone decides.
A program may use at most 64 MiB of HBM per device.

v0:
```python
import jax
import jax.numpy as jnp
from jax import lax
from jax.sharding import PartitionSpec as P

ITERS = 2


def from_root(value, axis, source):
    kept = jnp.where(lax.axis_index(axis) == source, value, 0).astype(value.dtype)
    return lax.psum(kept, axis)


def on_device(right_sides, nugget, cov_blocks, block_rows, block_cols, block_count):
    blocks = cov_blocks[0, 0].astype(jnp.float32)
    slot_rows = block_rows[0, 0]
    slot_cols = block_cols[0, 0]
    live_count = block_count[0, 0]
    slot_total = blocks.shape[0]
    tile_size = blocks.shape[1]
    series, row_width = right_sides.shape
    tile_count = row_width // tile_size
    live_mask = (jnp.arange(slot_total, dtype=jnp.int32) < live_count).astype(jnp.float32)
    block_ids = jnp.arange(tile_count, dtype=jnp.int32)[:, None]
    row_selector = (slot_rows[None, :] == block_ids).astype(jnp.float32) * live_mask[None, :]
    col_selector = (slot_cols[None, :] == block_ids).astype(jnp.float32) * live_mask[None, :]

    def spread(selector, values):
        placed = jnp.einsum("bm,rmj->rbj", selector, values, precision=lax.Precision.HIGHEST)
        return placed.reshape(series, row_width)

    solution = jnp.zeros_like(right_sides)
    residual = right_sides
    direction = right_sides
    norm_now = lax.psum(jnp.sum(residual * residual, axis=1), "row")
    for turn_index in range(ITERS):
        far_rows = from_root(direction, "row", lax.axis_index("col"))
        near_tiles = direction.reshape(series, tile_count, tile_size)
        far_tiles = far_rows.reshape(series, tile_count, tile_size)
        local_direct = jnp.einsum(
            "rmk,mjk->rmj",
            jnp.take(far_tiles, slot_cols, axis=1),
            blocks,
            precision=lax.Precision.HIGHEST,
        )
        local_mirror = jnp.einsum(
            "rmj,mjk->rmk",
            jnp.take(near_tiles, slot_rows, axis=1),
            blocks,
            precision=lax.Precision.HIGHEST,
        )
        apply_direct = spread(row_selector, local_direct)
        apply_mirror = spread(col_selector, local_mirror)
        total = lax.psum(apply_direct, "col")
        summed = lax.psum(apply_mirror, "row")
        total = total + from_root(summed, "col", lax.axis_index("row"))
        applied = nugget[None, :] * direction + total
        curvature, crossed, squared = lax.psum(
            (
                jnp.sum(direction * applied, axis=1),
                jnp.sum(residual * applied, axis=1),
                jnp.sum(applied * applied, axis=1),
            ),
            "row",
        )
        step_size = norm_now / curvature
        solution = solution + step_size[:, None] * direction
        residual = residual - step_size[:, None] * applied
        norm_next = norm_now - 2.0 * step_size * crossed + step_size * step_size * squared
        direction = residual + (norm_next / norm_now)[:, None] * direction
        norm_now = norm_next
    return (solution, residual)


def solution(mesh):
    placed = (
        P(None, ("groups", "row")),
        P(("groups", "row")),
        P(("groups", "row"), "col", None, None, None),
        P(("groups", "row"), "col", None),
        P(("groups", "row"), "col", None),
        P(("groups", "row"), "col"),
    )
    return jax.shard_map(
        on_device,
        mesh=mesh,
        in_specs=placed,
        out_specs=(P(None, ("groups", "row")), P(None, ("groups", "row"))),
        check_vma=False,
    )
```

profile of v0, /device:TPU:0, one launch (start us, length us, event | category | flops | bytes accessed | tf_op | source)
XLA Modules:
  0.0 210.6 jit_solution(2557300919919235164)
XLA Ops:
  7.2 0.0 all-reduce.14.cloned.1.call-start
  7.2 0.7 compare_and_fusion
  7.9 0.7 compare_select_fusion
  9.2 1.0 copy.38
  10.2 1.0 broadcast_select_fusion.1
  11.2 0.7 copy.39
  11.9 0.0 copy-start.5
  11.9 0.6 gather_fusion.1
  12.5 4.4 %fusion.11 = f32[32,32,256]{2,0,1:T(8,128)S(1)} fusion(bf16[1,1,32,256,256]{4,3,2,1,0:T(8,128)(2,1)} %param.10, f32[32,32,256]{2,1,0:T(8,128)S(1)} %gather_fusion.1, pred[32]{0:T(512)(128)(4,1)S(1)} %compare_and_fusion), kind=kOutput, calls=%fused_computation.13 | convolution fusion | flops 805568512 | bytes 6291488 | tf_op jit(solution)/shard_map/rmj,mjk->rmk/dot_general | solution.py:46
  16.9 0.0 copy-done.5
  16.9 1.2 fusion.28
  18.2 0.8 copy.21
  18.9 0.0 all-reduce.14.cloned.1.call-update
  19.0 0.0 all-reduce.8.cloned.1.call-start
  19.1 35.7 %all-reduce.14.cloned.1.call-done = (f32[32,8,256]{2,0,1:T(8,128)}, f32[32,2048]{1,0:T(8,128)}) async-done(((f32[32,8,256]{2,0,1:T(8,128)}, f32[32,2048]{1,0:T(8,128)}), (f32[32,8,256]{2,0,1:T(8,128)}, f32[32,2048]{1,0:T(8,128)})) %all-reduce.14.cloned.1.call-update) | async-done | bytes 524304 | tf_op jit(solution)/shard_map/psum | solution.py:11
  54.8 0.0 copy-start.6
  54.8 1.6 gather_fusion
  56.4 0.0 copy-start.2
  56.4 0.0 copy-start
  56.4 0.0 copy-start.4
  56.4 6.0 %fusion.8 = f32[32,32,256]{2,0,1:T(8,128)S(1)} fusion(bf16[1,1,32,256,256]{4,3,2,1,0:T(8,128)(2,1)} %param.10, f32[32,32,256]{2,1,0:T(8,128)S(1)} %gather_fusion, pred[32]{0:T(512)(128)(4,1)S(1)} %compare_and_fusion.1), kind=kOutput, calls=%fused_computation.12 | convolution fusion | flops 805568512 | bytes 6291488 | tf_op jit(solution)/shard_map/rmk,mjk->rmj/dot_general | solution.py:40
  62.4 0.0 copy-done.6
  62.4 1.2 fusion.30
  63.7 0.1 copy.20
  63.7 0.0 copy-done.2
  63.8 0.7 select_add_fusion.1
  64.5 0.0 all-reduce.8.cloned.1.call-update
  64.5 0.0 all-reduce.12.cloned.1.call-start
  64.6 35.8 %all-reduce.8.cloned.1.call-done = f32[32,2048]{1,0:T(8,128)} async-done(((f32[32,2048]{1,0:T(8,128)}), f32[32,2048]{1,0:T(8,128)}) %all-reduce.8.cloned.1.call-update) | async-done | bytes 262160 | tf_op jit(solution)/shard_map/psum | solution.py:54
  100.4 0.0 copy-done
  100.4 0.0 copy-done.4
  100.4 1.2 multiply_reduce_fusion.2
  101.6 5.7 %all-reduce = (f32[32]{0:T(128)S(1)}, f32[32]{0:T(128)S(1)}, f32[32]{0:T(128)S(1)}) all-reduce(f32[32]{0:T(128)S(1)} %get-tuple-element.4, f32[32]{0:T(128)S(1)} %get-tuple-element.5, f32[32]{0:T(128)S(1)} %get-tuple-element.3), channel_id=1, replica_groups=mesh['groups'=2,'row'=4,'col'=4] {'row'}, use_global_device_ids=true, to_apply=%region_9.11 | all-reduce | flops 96 | bytes 768 | tf_op jit(solution)/shard_map/psum | solution.py:58
  107.3 1.1 broadcast_select_fusion
  108.3 0.7 copy.37
  109.1 0.6 gather_fusion.3
  109.7 4.4 %fusion.17 = f32[32,32,256]{2,0,1:T(8,128)S(1)} fusion(bf16[1,1,32,256,256]{4,3,2,1,0:T(8,128)(2,1)} %param.10, f32[32,32,256]{2,1,0:T(8,128)S(1)} %gather_fusion.3, pred[32]{0:T(512)(128)(4,1)S(1)} %compare_and_fusion), kind=kOutput, calls=%fused_computation.15 | convolution fusion | flops 805568512 | bytes 6291488 | tf_op jit(solution)/shard_map/rmj,mjk->rmk/dot_general | solution.py:46
  114.1 1.2 fusion.24
  115.3 0.8 copy.23
  116.1 0.0 all-reduce.12.cloned.1.call-update
  116.1 0.2 all-reduce.10.cloned.1.call-start
  116.4 33.5 %all-reduce.12.cloned.1.call-done = (f32[32,8,256]{2,0,1:T(8,128)}, f32[32,2048]{1,0:T(8,128)}) async-done(((f32[32,8,256]{2,0,1:T(8,128)}, f32[32,2048]{1,0:T(8,128)}), (f32[32,8,256]{2,0,1:T(8,128)}, f32[32,2048]{1,0:T(8,128)})) %all-reduce.12.cloned.1.call-update) | async-done | bytes 524304 | tf_op jit(solution)/shard_map/psum | solution.py:11
  149.9 1.6 gather_fusion.2
  151.5 0.0 copy-start.3
  151.5 0.0 copy-start.1
  151.5 6.0 %fusion.14 = f32[32,32,256]{2,0,1:T(8,128)S(1)} fusion(bf16[1,1,32,256,256]{4,3,2,1,0:T(8,128)(2,1)} %param.10, f32[32,32,256]{2,1,0:T(8,128)S(1)} %gather_fusion.2, pred[32]{0:T(512)(128)(4,1)S(1)} %compare_and_fusion.1), kind=kOutput, calls=%fused_computation.14 | convolution fusion | flops 805568512 | bytes 6291488 | tf_op jit(solution)/shard_map/rmk,mjk->rmj/dot_general | solution.py:40
  157.5 1.2 fusion.26
  158.7 0.1 copy.22
  158.8 0.0 copy-done.3
  158.8 0.7 select_add_fusion
  159.6 0.0 all-reduce.10.cloned.1.call-update
  159.6 35.9 %all-reduce.10.cloned.1.call-done = f32[32,2048]{1,0:T(8,128)} async-done(((f32[32,2048]{1,0:T(8,128)}), f32[32,2048]{1,0:T(8,128)}) %all-reduce.10.cloned.1.call-update) | async-done | bytes 262160 | tf_op jit(solution)/shard_map/psum | solution.py:54
  195.4 1.1 multiply_reduce_fusion
  196.5 5.7 %psum.98 = f32[32]{0:T(128)S(1)} all-reduce(f32[32]{0:T(128)S(1)} %multiply_reduce_fusion), channel_id=1, replica_groups=mesh['groups'=2,'row'=4,'col'=4] {'row'}, use_global_device_ids=true, to_apply=%region_15.17 | all-reduce | flops 32 | bytes 256 | tf_op jit(solution)/shard_map/psum | solution.py:58
  202.2 0.0 copy-done.1
  202.2 1.9 multiply_subtract_fusion
  (8 shorter events, 0.1 us)
Async XLA Ops:
  7.2 47.6 %all-reduce.14.cloned.1.call-start = ((), (), s32[]{:S(2)}) async-start(), calls=%async_computation.3 | async-start | bytes 1048576 | tf_op jit(solution)/shard_map/psum | solution.py:11
  11.9 5.0 %copy-start.5 = (s32[1,1,32]{2,1,0:T(1,128)S(1)}, s32[1,1,32]{2,1,0:T(1,128)}, u32[]{:S(2)}) copy-start(s32[1,1,32]{2,1,0:T(1,128)} %param.12) | copy-start | bytes 388
  19.0 81.4 %all-reduce.8.cloned.1.call-start = ((), (), s32[]{:S(2)}) async-start(), calls=%async_computation | async-start | bytes 524288 | tf_op jit(solution)/shard_map/psum | solution.py:54
  54.8 7.6 %copy-start.6 = (s32[1,1,32]{2,1,0:T(1,128)S(1)}, s32[1,1,32]{2,1,0:T(1,128)}, u32[]{:S(2)}) copy-start(s32[1,1,32]{2,1,0:T(1,128)} %param.11) | copy-start | bytes 388
  56.4 7.4 %copy-start.2 = (f32[32,2048]{1,0:T(8,128)S(1)}, f32[32,2048]{1,0:T(8,128)}, u32[]{:S(2)}) copy-start(f32[32,2048]{1,0:T(8,128)} %get-tuple-element.12) | copy-start | bytes 786436
  56.4 44.0 %copy-start = (f32[32,2048]{1,0:T(8,128)S(1)}, f32[32,2048]{1,0:T(8,128)}, u32[]{:S(2)}) copy-start(f32[32,2048]{1,0:T(8,128)} %param.8) | copy-start | bytes 786436
  56.4 44.0 %copy-start.4 = (f32[2048]{0:T(1024)S(1)}, f32[2048]{0:T(1024)}, u32[]{:S(2)}) copy-start(f32[2048]{0:T(1024)} %param.9) | copy-start | bytes 24580
  64.5 85.4 %all-reduce.12.cloned.1.call-start = ((), (), s32[]{:S(2)}) async-start(), calls=%async_computation.2 | async-start | bytes 1048576 | tf_op jit(solution)/shard_map/psum | solution.py:11
  116.1 79.3 %all-reduce.10.cloned.1.call-start = ((), (), s32[]{:S(2)}) async-start(), calls=%async_computation.1 | async-start | bytes 524288 | tf_op jit(solution)/shard_map/psum | solution.py:54
  151.5 7.4 %copy-start.3 = (f32[32,2048]{1,0:T(8,128)S(1)}, f32[32,2048]{1,0:T(8,128)}, u32[]{:S(2)}) copy-start(f32[32,2048]{1,0:T(8,128)} %get-tuple-element.10) | copy-start | bytes 786436
  151.5 50.7 %copy-start.1 = (f32[32,2048]{1,0:T(8,128)S(1)}, f32[32,2048]{1,0:T(8,128)}, u32[]{:S(2)}) copy-start(f32[32,2048]{1,0:T(8,128)} %all-reduce.8.cloned.1.call-done) | copy-start | bytes 786436
Sparse Core Ops, SparseCore 0:
  19.1 35.6 all-reduce.13
  64.6 35.7 all-reduce.7
  116.3 33.5 all-reduce.11
  159.7 35.6 all-reduce.9
where the time goes:
time: 211 us
  waiting for transfers between devices  141 us (67%)
  matrix products  25.7 us (12%)
  between operations  14.7 us (7%)
  blocking collectives  11.3 us (5%)
  other arithmetic  9.03 us (4%)
  local copies, waits for them, and re-layouts  8.58 us (4%)
    psum x2, waiting for transfers between devices, on_device(): total = lax.psum(apply_direct, 'col')  71.7 us
    psum x2, waiting for transfers between devices, from_root(): return lax.psum(kept, axis)  69.2 us
    dot_general x2, matrix products, on_device(): jnp.einsum('rmk,mjk->rmj', jnp.take(far_tiles, slot_cols, axis=1), blocks...  12 us
    psum x2, blocking collectives, on_device(): lax.psum((jnp.sum(direction * applied, axis=1), jnp.sum(residual * applie...  11.3 us
    dot_general x2, matrix products, on_device(): jnp.einsum('rmj,mjk->rmk', jnp.take(near_tiles, slot_rows, axis=1), block...  8.74 us
    dot_general x4, matrix products, spread(): jnp.einsum('bm,rmj->rbj', selector, values, precision=lax.Precision.HIGHEST)  4.95 us
  transfers between devices with their start and end apart: 4, of which 4 were waited for; matrix products, arithmetic and copies ran while one was open for 0% of the time, Pallas kernels for 0%

commit v1 on v0

--- a/solution.py
+++ b/solution.py
@@ -8,7 +8,7 @@
 
 def from_root(value, axis, source):
     kept = jnp.where(lax.axis_index(axis) == source, value, 0).astype(value.dtype)
-    return lax.psum(kept, axis)
+    return jnp.sum(lax.all_gather(kept, axis), axis=0)
 
 
 def on_device(right_sides, nugget, cov_blocks, block_rows, block_cols, block_count):

time: 211 us -> 290 us (1.37)
  waiting for transfers between devices: 141 us -> 214 us
  other arithmetic: 9.03 us -> 15.6 us
    all_gather x0 -> x4, waiting for transfers between devices: none -> 74.2 us  [from_root(): return jnp.sum(lax.all_gather(kept, axis), axis=0)]
    reduce_sum x0 -> x4, other arithmetic: none -> 5.22 us  [from_root(): return jnp.sum(lax.all_gather(kept, axis), axis=0)]
    psum x2, waiting for transfers between devices: 69.2 us -> 66.2 us  [on_device(): summed = lax.psum(apply_mirror, 'row')]
  transfers between devices with their start and end apart: 4 -> 8, of which waited for: 4 -> 8; matrix products, arithmetic and copies ran while one was open for 0% -> 9% of each run, Pallas kernels for 0% -> 0%
where the time goes in v1:
time: 290 us; the launch traced here: 289 us
  waiting for transfers between devices  214 us (74%)
  matrix products  25.6 us (9%)
  other arithmetic  15.6 us (5%)
  between operations  15 us (5%)
  blocking collectives  11.3 us (4%)
  local copies, waits for them, and re-layouts  6.66 us (2%)
    all_gather x4, waiting for transfers between devices, from_root(): return jnp.sum(lax.all_gather(kept, axis), axis=0)  74.2 us
    psum x2, waiting for transfers between devices, on_device(): total = lax.psum(apply_direct, 'col')  73 us
    psum x2, waiting for transfers between devices, on_device(): summed = lax.psum(apply_mirror, 'row')  66.2 us
    dot_general x2, matrix products, on_device(): jnp.einsum('rmk,mjk->rmj', jnp.take(far_tiles, slot_cols, axis=1), blocks...  11.9 us
    psum x2, blocking collectives, on_device(): lax.psum((jnp.sum(direction * applied, axis=1), jnp.sum(residual * applie...  11.3 us
    dot_general x2, matrix products, on_device(): jnp.einsum('rmj,mjk->rmk', jnp.take(near_tiles, slot_rows, axis=1), block...  8.79 us
  transfers between devices with their start and end apart: 8, of which 8 were waited for; matrix products, arithmetic and copies ran while one was open for 9% of the time, Pallas kernels for 0%

profile of v1, /device:TPU:0, one launch (start us, length us, event | category | flops | bytes accessed | tf_op | source)
XLA Modules:
  0.0 288.9 jit_solution(11819316728385340539)
XLA Ops:
  7.2 0.0 all-reduce.8.cloned.1.call-start
  7.2 0.7 compare_select_fusion
  7.9 0.7 compare_and_fusion
  9.2 1.0 copy.38
  10.2 0.0 copy-start.2
  10.2 0.6 gather_fusion.1
  10.8 0.0 copy-start
  10.8 4.4 %fusion.11 = f32[32,32,256]{2,0,1:T(8,128)S(1)} fusion(bf16[1,1,32,256,256]{4,3,2,1,0:T(8,128)(2,1)} %param.10, f32[32,32,256]{2,1,0:T(8,128)S(1)} %gather_fusion.1, pred[32]{0:T(512)(128)(4,1)S(1)} %compare_and_fusion), kind=kOutput, calls=%fused_computation.13 | convolution fusion | flops 805568512 | bytes 6291488 | tf_op jit(solution)/shard_map/rmj,mjk->rmk/dot_general | solution.py:46
  15.3 0.0 copy-done.2
  15.3 1.2 fusion.28
  16.5 0.8 copy.21
  17.3 0.0 all-reduce.8.cloned.1.call-update
  17.3 0.0 all-gather.9.cloned.1.call-start
  17.4 0.0 copy-done
  17.4 0.7 broadcast_select_fusion.3
  18.1 0.0 all-gather.9.cloned.1.call-update
  18.1 0.0 all-gather.11.cloned.1.call-start
  18.2 34.3 %all-reduce.8.cloned.1.call-done = f32[32,2048]{1,0:T(8,128)} async-done(((f32[32,2048]{1,0:T(8,128)}), f32[32,2048]{1,0:T(8,128)}) %all-reduce.8.cloned.1.call-update) | async-done | bytes 262160 | tf_op jit(solution)/shard_map/psum | solution.py:55
  52.5 1.7 broadcast_select_fusion.2
  54.2 0.0 all-gather.11.cloned.1.call-update
  54.2 0.0 all-reduce.6.cloned.1.call-start
  54.3 17.1 %all-gather.9.cloned.1.call-done = f32[128,2048]{1,0:T(8,128)} async-done(((f32[32,2048]{1,0:T(8,128)}), f32[128,2048]{1,0:T(8,128)}) %all-gather.9.cloned.1.call-update) | async-done | bytes 1048592 | tf_op jit(solution)/shard_map/all_gather | solution.py:11
  71.4 1.3 reduce_sum.77
  72.7 0.0 copy-start.3
  72.7 0.6 gather_fusion
  73.3 0.0 copy-start.1
  73.3 5.9 %fusion.8 = f32[32,32,256]{2,0,1:T(8,128)S(1)} fusion(bf16[1,1,32,256,256]{4,3,2,1,0:T(8,128)(2,1)} %param.10, f32[32,32,256]{2,1,0:T(8,128)S(1)} %gather_fusion, pred[32]{0:T(512)(128)(4,1)S(1)} %compare_and_fusion.1), kind=kOutput, calls=%fused_computation.12 | convolution fusion | flops 805568512 | bytes 6291488 | tf_op jit(solution)/shard_map/rmk,mjk->rmj/dot_general | solution.py:40
  79.3 0.0 copy-done.3
  79.3 1.2 fusion.30
  80.5 0.8 copy.20
  81.3 0.0 all-reduce.6.cloned.1.call-update
  81.4 0.0 all-reduce.12.cloned.1.call-start
  81.4 20.1 %all-gather.11.cloned.1.call-done = f32[128,2048]{1,0:T(8,128)} async-done(((f32[32,2048]{1,0:T(8,128)}), f32[128,2048]{1,0:T(8,128)}) %all-gather.11.cloned.1.call-update) | async-done | bytes 1048592 | tf_op jit(solution)/shard_map/all_gather | solution.py:11
  101.5 1.3 reduce_sum.78
  102.8 36.5 %all-reduce.6.cloned.1.call-done = f32[32,2048]{1,0:T(8,128)} async-done(((f32[32,2048]{1,0:T(8,128)}), f32[32,2048]{1,0:T(8,128)}) %all-reduce.6.cloned.1.call-update) | async-done | bytes 262160 | tf_op jit(solution)/shard_map/psum | solution.py:54
  139.3 0.0 copy-done.1
  139.3 1.2 multiply_reduce_fusion.2
  140.5 5.7 %all-reduce = (f32[32]{0:T(128)S(1)}, f32[32]{0:T(128)S(1)}, f32[32]{0:T(128)S(1)}) all-reduce(f32[32]{0:T(128)S(1)} %get-tuple-element.4, f32[32]{0:T(128)S(1)} %get-tuple-element.5, f32[32]{0:T(128)S(1)} %get-tuple-element.3), channel_id=1, replica_groups=mesh['groups'=2,'row'=4,'col'=4] {'row'}, use_global_device_ids=true, to_apply=%region_9.11 | all-reduce | flops 96 | bytes 768 | tf_op jit(solution)/shard_map/psum | solution.py:58
  146.2 0.8 broadcast_select_fusion.1
  147.0 0.6 gather_fusion.3
  147.6 4.4 %fusion.17 = f32[32,32,256]{2,0,1:T(8,128)S(1)} fusion(bf16[1,1,32,256,256]{4,3,2,1,0:T(8,128)(2,1)} %param.10, f32[32,32,256]{2,1,0:T(8,128)S(1)} %gather_fusion.3, pred[32]{0:T(512)(128)(4,1)S(1)} %compare_and_fusion), kind=kOutput, calls=%fused_computation.15 | convolution fusion | flops 805568512 | bytes 6291488 | tf_op jit(solution)/shard_map/rmj,mjk->rmk/dot_general | solution.py:46
  152.0 1.2 fusion.24
  153.3 0.8 copy.23
  154.0 0.0 all-reduce.12.cloned.1.call-update
  154.1 0.0 all-gather.13.cloned.1.call-start
  154.1 0.5 all-gather.13.cloned.1.call-update
  154.6 0.0 all-gather.15.cloned.1.call-start
  154.7 31.9 %all-reduce.12.cloned.1.call-done = f32[32,2048]{1,0:T(8,128)} async-done(((f32[32,2048]{1,0:T(8,128)}), f32[32,2048]{1,0:T(8,128)}) %all-reduce.12.cloned.1.call-update) | async-done | bytes 262160 | tf_op jit(solution)/shard_map/psum | solution.py:55
  186.6 1.7 broadcast_select_fusion
  188.3 0.0 all-gather.15.cloned.1.call-update
  188.3 0.2 all-reduce.10.cloned.1.call-start
  188.6 16.8 %all-gather.13.cloned.1.call-done = f32[128,2048]{1,0:T(8,128)} async-done(((f32[32,2048]{1,0:T(8,128)}), f32[128,2048]{1,0:T(8,128)}) %all-gather.13.cloned.1.call-update) | async-done | bytes 1048592 | tf_op jit(solution)/shard_map/all_gather | solution.py:11
  205.4 1.3 reduce_sum.81
  206.7 0.6 gather_fusion.2
  207.3 5.9 %fusion.14 = f32[32,32,256]{2,0,1:T(8,128)S(1)} fusion(bf16[1,1,32,256,256]{4,3,2,1,0:T(8,128)(2,1)} %param.10, f32[32,32,256]{2,1,0:T(8,128)S(1)} %gather_fusion.2, pred[32]{0:T(512)(128)(4,1)S(1)} %compare_and_fusion.1), kind=kOutput, calls=%fused_computation.14 | convolution fusion | flops 805568512 | bytes 6291488 | tf_op jit(solution)/shard_map/rmk,mjk->rmj/dot_general | solution.py:40
  213.3 1.2 fusion.26
  214.5 0.8 copy.22
  215.3 0.0 all-reduce.10.cloned.1.call-update
  215.3 20.2 %all-gather.15.cloned.1.call-done = f32[128,2048]{1,0:T(8,128)} async-done(((f32[32,2048]{1,0:T(8,128)}), f32[128,2048]{1,0:T(8,128)}) %all-gather.15.cloned.1.call-update) | async-done | bytes 1048592 | tf_op jit(solution)/shard_map/all_gather | solution.py:11
  235.5 1.3 reduce_sum.82
  236.8 36.6 %all-reduce.10.cloned.1.call-done = f32[32,2048]{1,0:T(8,128)} async-done(((f32[32,2048]{1,0:T(8,128)}), f32[32,2048]{1,0:T(8,128)}) %all-reduce.10.cloned.1.call-update) | async-done | bytes 262160 | tf_op jit(solution)/shard_map/psum | solution.py:54
  273.4 1.1 multiply_reduce_fusion
  274.5 5.7 %psum.66 = f32[32]{0:T(128)S(1)} all-reduce(f32[32]{0:T(128)S(1)} %multiply_reduce_fusion), channel_id=1, replica_groups=mesh['groups'=2,'row'=4,'col'=4] {'row'}, use_global_device_ids=true, to_apply=%region_15.17 | all-reduce | flops 32 | bytes 256 | tf_op jit(solution)/shard_map/psum | solution.py:58
  280.2 1.9 multiply_subtract_fusion
  (10 shorter events, 0.1 us)
Async XLA Ops:
  7.2 45.3 %all-reduce.8.cloned.1.call-start = ((), (), s32[]{:S(2)}) async-start(), calls=%async_computation.1 | async-start | bytes 524288 | tf_op jit(solution)/shard_map/psum | solution.py:55
  10.2 5.1 %copy-start.2 = (s32[1,1,32]{2,1,0:T(1,128)S(1)}, s32[1,1,32]{2,1,0:T(1,128)}, u32[]{:S(2)}) copy-start(s32[1,1,32]{2,1,0:T(1,128)} %param.12) | copy-start | bytes 388
  10.8 6.6 %copy-start = (f32[32,2048]{1,0:T(8,128)S(1)}, f32[32,2048]{1,0:T(8,128)}, u32[]{:S(2)}) copy-start(f32[32,2048]{1,0:T(8,128)} %param.8) | copy-start | bytes 786436
  17.3 54.0 %all-gather.9.cloned.1.call-start = ((), (), s32[]{:S(2)}) async-start(), calls=%async_computation.4 | async-start | bytes 1310720 | tf_op jit(solution)/shard_map/all_gather | solution.py:11
  18.1 83.4 %all-gather.11.cloned.1.call-start = ((), (), s32[]{:S(2)}) async-start(), calls=%async_computation.5 | async-start | bytes 1310720 | tf_op jit(solution)/shard_map/all_gather | solution.py:11
  54.2 85.1 %all-reduce.6.cloned.1.call-start = ((), (), s32[]{:S(2)}) async-start(), calls=%async_computation | async-start | bytes 524288 | tf_op jit(solution)/shard_map/psum | solution.py:54
  72.7 6.6 %copy-start.3 = (s32[1,1,32]{2,1,0:T(1,128)S(1)}, s32[1,1,32]{2,1,0:T(1,128)}, u32[]{:S(2)}) copy-start(s32[1,1,32]{2,1,0:T(1,128)} %param.11) | copy-start | bytes 388
  73.3 66.0 %copy-start.1 = (f32[2048]{0:T(1024)S(1)}, f32[2048]{0:T(1024)}, u32[]{:S(2)}) copy-start(f32[2048]{0:T(1024)} %param.9) | copy-start | bytes 24580
  81.4 105.3 %all-reduce.12.cloned.1.call-start = ((), (), s32[]{:S(2)}) async-start(), calls=%async_computation.3 | async-start | bytes 524288 | tf_op jit(solution)/shard_map/psum | solution.py:55
  154.1 51.3 %all-gather.13.cloned.1.call-start = ((), (), s32[]{:S(2)}) async-start(), calls=%async_computation.6 | async-start | bytes 1310720 | tf_op jit(solution)/shard_map/all_gather | solution.py:11
  154.6 80.9 %all-gather.15.cloned.1.call-start = ((), (), s32[]{:S(2)}) async-start(), calls=%async_computation.7 | async-start | bytes 1310720 | tf_op jit(solution)/shard_map/all_gather | solution.py:11
  188.3 85.1 %all-reduce.10.cloned.1.call-start = ((), (), s32[]{:S(2)}) async-start(), calls=%async_computation.2 | async-start | bytes 524288 | tf_op jit(solution)/shard_map/psum | solution.py:54
Sparse Core Ops, SparseCore 0:
  17.4 35.0 all-reduce.7
  54.6 16.6 all-gather.8
  73.5 27.9 all-gather.10
  104.3 34.9 all-reduce.5
  154.2 32.3 all-reduce.11
  188.6 16.6 all-gather.12
  207.5 27.9 all-gather.14
  238.4 34.9 all-reduce.9
